TPU v7x, 32 devices: a whole 2x2x4 slice. The times are simulated.
32 devices in a mesh: rep: 8 (over z, y), zero: 4 (over x, core).
Axes of the slice: x: 2, y: 2, z: 4, core: 2. Of those that a mesh axis runs over, the one named last changes fastest.
Arguments:
- tokens: bfloat16 [12288, 1280], P(('rep', 'zero')), may hold values from -6 to 6
- cotangent: bfloat16 [12288, 1280], P(('rep', 'zero')), may hold values from -6 to 6
- weights: bfloat16 [1280, 6, 1280], P('zero')
- vectors: bfloat16 [5, 1280], P(None, 'zero')
- error: float32 [10240, 6, 1280], P(('rep', 'zero'))
- previous_right_factors: float32 [6, 1280, 32], P(None, None, 'zero'), may hold values from -6 to 6
- momentum: float32 [1280, 6, 1280], P('zero', None, 'rep')
- vec_momentum: float32 [5, 1280], P(None, 'zero')
- prompt_len: int32 [8], P('rep'), may hold values from 512 to 1024, as said below
Outputs:
- result: bfloat16 [12288, 1280], P(('rep', 'zero'))
- grad_tokens: float32 [12288, 1280], P(('rep', 'zero'))
- grad_weights: float32 [1280, 6, 1280], P('zero', None, 'rep')
- grad_vectors: float32 [5, 1280], P(None, 'zero')
- new_error: float32 [10240, 6, 1280], P(('rep', 'zero'))
- fresh_right_factors: float32 [6, 1280, 32], P(None, None, 'zero')
- new_momentum: float32 [1280, 6, 1280], P('zero', None, 'rep')
- new_vec_momentum: float32 [5, 1280], P(None, 'zero')
- update_weights: float32 [1280, 6, 1280], P('zero', None, 'rep')
- update_vectors: float32 [5, 1280], P(None, 'zero')
Inputs may be any that keep to these rules, and one draw needn't show every extreme that they name: `prompt_len`: valid prompt rows of a group; the other prompt rows of its 1024 are padding.
All inputs are finite; a program needn't handle non-finite values.
Results may differ from a plain program's by a relative error of at most 0.028.
Values may be sent and summed in bfloat16 or wider, within the bound.
No kernel may reach another device: no remote copies, remote signals or barrier semaphores. Data moves between devices by JAX's collectives and lax.ppermute only.
A program may use at most 320 MiB of HBM per device.

v0:
```python
import math
import jax
import jax.numpy as jnp
from jax import lax
from jax.sharding import PartitionSpec as P

HEADS = 16
PROMPT = 1024
EPS = 1e-06
MU = 0.9
LOG2E = 1.442695041
NEG = -1e30
PRECISION_HIGH = lax.Precision.HIGHEST


def rms_scale(field):
    return lax.rsqrt(jnp.mean(field * field, axis=-1, keepdims=True) + EPS)


def norm_back(field, scale, gain_vec, grad_in):
    weighted = grad_in * gain_vec
    inner = jnp.mean(field * weighted, axis=-1, keepdims=True)
    return scale * weighted - field * (scale * scale * scale) * inner


def orthonormal(factor):
    columns = []
    for col_index in range(factor.shape[-1]):
        column = factor[..., col_index]
        for earlier in columns:
            column = column - jnp.sum(earlier * column, axis=-2, keepdims=True) * earlier
        column = column * lax.rsqrt(jnp.sum(column * column, axis=-2, keepdims=True) + EPS)
        columns.append(column)
    return jnp.stack(columns, axis=-1)


def on_device(
    tokens,
    cotangent,
    weights,
    vectors,
    error,
    previous_right_factors,
    momentum,
    vec_momentum,
    prompt_len,
):
    f32 = jnp.float32
    bf16 = jnp.bfloat16
    zero_index = lax.axis_index("zero")
    rep_index = lax.axis_index("rep")
    zero_count = lax.axis_size("zero")
    rep_count = lax.axis_size("rep")
    tok_rows, feat_width = tokens.shape
    head_dim = feat_width // HEADS
    prompt_rows = PROMPT // zero_count
    prompt_valid = prompt_len[0]
    full_w, full_v = (
        lax.all_gather(weights, "zero", axis=0, tiled=True),
        lax.all_gather(vectors, "zero", axis=1, tiled=True),
    )
    vec_float = full_v.astype(f32)
    gain_one = vec_float[0]
    gain_two = vec_float[1]
    bias_one = vec_float[2]
    bias_two = vec_float[3]
    scale_raw = vec_float[4]
    tok_float = tokens.astype(f32)
    scale_one = rms_scale(tok_float)
    normed_one = (tok_float * scale_one * gain_one).astype(bf16)
    projected = jnp.einsum("ti,omi->mto", normed_one, full_w[:, 0:3, :], preferred_element_type=f32)
    query = projected[0]
    key_low = projected[1].astype(bf16)
    value_low = projected[2].astype(bf16)
    scale_const = LOG2E / math.sqrt(head_dim)
    query_scale = scale_const * jax.nn.softplus(scale_raw)
    scaled = (query * query_scale).astype(bf16)
    key_far, value_far = (
        lax.all_gather(key_low[:prompt_rows], "zero", axis=0, tiled=True),
        lax.all_gather(value_low[:prompt_rows], "zero", axis=0, tiled=True),
    )
    key_rows = jnp.concatenate([key_far, key_low[prompt_rows:]], axis=0)
    value_rows = jnp.concatenate([value_far, value_low[prompt_rows:]], axis=0)
    key_count = key_rows.shape[0]
    q_row = lax.broadcasted_iota(jnp.int32, (tok_rows, key_count), 0)
    k_col = lax.broadcasted_iota(jnp.int32, (tok_rows, key_count), 1)
    q_prompt = q_row < prompt_rows
    q_pos = zero_index * prompt_rows + q_row
    k_prompt = k_col < PROMPT
    see_prompt = k_prompt & (k_col < prompt_valid) & (jnp.logical_not(q_prompt) | (k_col <= q_pos))
    see_cont = (
        jnp.logical_not(k_prompt)
        & jnp.logical_not(q_prompt)
        & (k_col - PROMPT <= q_row - prompt_rows)
    )
    allowed = see_prompt | see_cont
    q_heads = scaled.reshape(tok_rows, HEADS, head_dim)
    k_heads = key_rows.reshape(key_count, HEADS, head_dim)
    v_heads = value_rows.reshape(key_count, HEADS, head_dim)

    def masked_scores():
        raw_scores = jnp.einsum("thd,khd->htk", q_heads, k_heads, preferred_element_type=f32)
        return jnp.where(allowed[None], raw_scores, NEG)

    masked = masked_scores()
    row_top = jnp.max(masked, axis=-1, keepdims=True)
    log_total = row_top + jnp.log(jnp.sum(jnp.exp(masked - row_top), axis=-1, keepdims=True))
    probs = jnp.exp(masked - log_total)
    attended = (
        jnp.einsum("htk,khd->thd", probs.astype(bf16), v_heads, preferred_element_type=f32)
        .reshape(tok_rows, feat_width)
        .astype(bf16)
    )
    branch = jnp.einsum("ti,oi->to", attended, full_w[:, 3, :], preferred_element_type=f32)
    hidden = tok_float + branch
    scale_two = rms_scale(hidden)
    normed_two = (hidden * scale_two * gain_two).astype(bf16)
    upper = (
        jnp.einsum("ti,oi->to", normed_two, full_w[:, 4, :], preferred_element_type=f32) + bias_one
    )
    activ = jax.nn.silu(upper).astype(bf16)
    output = jnp.einsum("ti,oi->to", activ, full_w[:, 5, :], preferred_element_type=f32) + bias_two
    result = (hidden + output).astype(bf16)
    back_w = lax.all_gather(weights, "zero", axis=0, tiled=True)
    grad_out = cotangent.astype(f32)
    grad_f = grad_out.astype(bf16)
    grad_act = jnp.einsum("to,oi->ti", grad_f, back_w[:, 5, :], preferred_element_type=f32)
    gate_sig = jax.nn.sigmoid(upper)
    grad_up = (grad_act * gate_sig * (1.0 + upper * (1.0 - gate_sig))).astype(bf16)
    grad_n2 = jnp.einsum("to,oi->ti", grad_up, back_w[:, 4, :], preferred_element_type=f32)
    grad_gain_two = jnp.sum(grad_n2 * hidden * scale_two, axis=0)
    grad_hidden = grad_out + norm_back(hidden, scale_two, gain_two, grad_n2)
    grad_branch = grad_hidden.astype(bf16)
    grad_att = jnp.einsum(
        "to,oi->ti", grad_branch, back_w[:, 3, :], preferred_element_type=f32
    ).astype(bf16)
    grad_att_heads = grad_att.reshape(tok_rows, HEADS, head_dim)
    probs_again = jnp.exp(masked_scores() - log_total)
    grad_probs = jnp.einsum("thd,khd->htk", grad_att_heads, v_heads, preferred_element_type=f32)
    delta = jnp.sum(probs_again * grad_probs, axis=-1, keepdims=True)
    grad_scores = (probs_again * (grad_probs - delta)).astype(bf16)
    grad_values = jnp.einsum(
        "htk,thd->khd", probs_again.astype(bf16), grad_att_heads, preferred_element_type=f32
    ).reshape(key_count, feat_width)
    grad_keys = jnp.einsum(
        "htk,thd->khd", grad_scores, q_heads, preferred_element_type=f32
    ).reshape(key_count, feat_width)
    grad_sq = jnp.einsum("htk,khd->thd", grad_scores, k_heads, preferred_element_type=f32).reshape(
        tok_rows, feat_width
    )
    own_keys, own_values = (
        lax.psum_scatter(
            grad_keys[:PROMPT].astype(jnp.bfloat16), "zero", scatter_dimension=0, tiled=True
        ).astype(jnp.float32),
        lax.psum_scatter(
            grad_values[:PROMPT].astype(jnp.bfloat16), "zero", scatter_dimension=0, tiled=True
        ).astype(jnp.float32),
    )
    grad_key = jnp.concatenate([own_keys, grad_keys[PROMPT:]], axis=0).astype(bf16)
    grad_value = jnp.concatenate([own_values, grad_values[PROMPT:]], axis=0).astype(bf16)
    grad_query = (grad_sq * query_scale).astype(bf16)
    grad_scale_raw = jnp.sum(grad_sq * query, axis=0) * scale_const * jax.nn.sigmoid(scale_raw)
    grad_proj = jnp.stack([grad_query, grad_key, grad_value], axis=0)
    grad_n1 = jnp.einsum("mto,omi->ti", grad_proj, back_w[:, 0:3, :], preferred_element_type=f32)
    grad_gain_one = jnp.sum(grad_n1 * tok_float * scale_one, axis=0)
    grad_tokens = grad_hidden + norm_back(tok_float, scale_one, gain_one, grad_n1)
    grad_stack = jnp.stack([grad_query, grad_key, grad_value, grad_branch, grad_up, grad_f], axis=0)
    input_stack = jnp.stack(
        [normed_one, normed_one, normed_one, attended, normed_two, activ], axis=0
    )
    grad_block = lax.psum_scatter(
        jnp.einsum("mto,mti->omi", grad_stack, input_stack, preferred_element_type=f32).astype(
            jnp.bfloat16
        ),
        "zero",
        scatter_dimension=0,
        tiled=True,
    ).astype(jnp.float32)
    vec_terms = jnp.stack(
        [
            grad_gain_one,
            grad_gain_two,
            jnp.sum(grad_up.astype(f32), axis=0),
            jnp.sum(grad_f.astype(f32), axis=0),
            grad_scale_raw,
        ],
        axis=0,
    )
    vec_block = lax.psum_scatter(vec_terms, "zero", scatter_dimension=1, tiled=True)
    combined_result = grad_block + error
    local_left_factor = jnp.einsum(
        "edn,dnw->edw", combined_result, previous_right_factors, precision=PRECISION_HIGH
    )
    vec_total = lax.psum(vec_block, "rep")
    left_parts = []
    right_parts = []
    for mat_index in range(combined_result.shape[1]):
        left_sum = lax.psum(local_left_factor[:, mat_index], "rep")
        left_ortho = orthonormal(left_sum[:, None, :] / rep_count)[:, 0, :]
        right_term = jnp.einsum(
            "oi,or->ir", combined_result[:, mat_index], left_ortho, precision=PRECISION_HIGH
        )
        right_parts.append(lax.psum(right_term.astype(jnp.bfloat16), "rep").astype(jnp.float32))
        left_parts.append(left_ortho)
    orthogonalized = jnp.stack(left_parts, axis=1)
    right_total = jnp.stack(right_parts, axis=0)
    fresh_right_factors = right_total / rep_count
    approximation = jnp.einsum(
        "upt,pqt->upq", orthogonalized, fresh_right_factors, precision=PRECISION_HIGH
    )
    new_error = combined_result - approximation
    rep_width = feat_width // rep_count
    grad_weights = lax.dynamic_slice_in_dim(approximation, rep_index * rep_width, rep_width, 2)
    step_rate = 0.03 / math.sqrt(zero_count * tok_rows)
    new_momentum = MU * momentum + grad_weights
    update_weights = -step_rate * new_momentum
    grad_vectors = vec_total / rep_count
    new_vec_momentum = MU * vec_momentum + grad_vectors
    update_vectors = -step_rate * new_vec_momentum
    return (
        result,
        grad_tokens,
        grad_weights,
        grad_vectors,
        new_error,
        fresh_right_factors,
        new_momentum,
        new_vec_momentum,
        update_weights,
        update_vectors,
    )


def solution(mesh):
    in_specs = (
        P(("rep", "zero"), None),
        P(("rep", "zero"), None),
        P("zero", None, None),
        P(None, "zero"),
        P(("rep", "zero"), None, None),
        P(None, None, "zero"),
        P("zero", None, "rep"),
        P(None, "zero"),
        P("rep"),
    )
    out_specs = (
        P(("rep", "zero"), None),
        P(("rep", "zero"), None),
        P("zero", None, "rep"),
        P(None, "zero"),
        P(("rep", "zero"), None, None),
        P(None, None, "zero"),
        P("zero", None, "rep"),
        P(None, "zero"),
        P("zero", None, "rep"),
        P(None, "zero"),
    )
    return jax.shard_map(
        on_device, mesh=mesh, in_specs=in_specs, out_specs=out_specs, check_vma=False
    )
```

profile of v0, /device:TPU:0, one launch (start us, length us, event | category | flops | bytes accessed | tf_op | source)
XLA Modules:
  0.0 1215.3 jit_solution(3644075702543074997)
XLA Ops:
  15.9 120.7 %all-gather.7.cloned.1.call-done = bf16[1280,6,1280]{2,0,1:T(8,128)(2,1)} async-done(((bf16[320,6,1280]{2,0,1:T(8,128)(2,1)}), bf16[1280,6,1280]{2,0,1:T(8,128)(2,1)}) %all-gather.7.cloned.1.call-update) | async-done | bytes 19660816 | tf_op jit(solution)/shard_map/all_gather | solution.py:59
  163.3 12.1 all-gather.9.cloned.1.call-done
  175.4 27.7 %all-gather.11.cloned.1.call-done = bf16[1,1024,1280]{2,1,0:T(8,128)(2,1)} async-done(((bf16[1,256,1280]{2,1,0:T(8,128)(2,1)}), bf16[1,1024,1280]{2,1,0:T(8,128)(2,1)}) %all-gather.11.cloned.1.call-update) | async-done | bytes 2621456 | tf_op jit(solution)/shard_map/all_gather | solution.py:79
  218.6 13.1 %select_reduce_fusion = (f32[16,384]{1,0:T(8,128)S(1)}, f32[16,384,1152]{2,1,0:T(8,128)}) fusion(pred[384,1152]{1,0:T(8,128)(4,1)} %fusion.50, bf16[1152,16,80]{0,2,1:T(8,128)(2,1)} %bitcast.662, f32[384,16,80]{0,2,1:T(8,128)S(1)} %bitcast.659, f32[16,80]{1,0:T(8,128)S(1)} %mul.16566), kind=kOutput, calls=%fused_computation.5 | convolution fusion | flops 1147594752 | bytes 33698816 | tf_op jit(solution)/shard_map/thd,khd->htk/dot_general | solution.py:102
  231.6 13.7 %exponential_reduce_fusion = f32[16,384]{1,0:T(8,128)S(1)} fusion(f32[16,384,1152]{2,1,0:T(8,128)} %get-tuple-element.459, f32[16,384]{1,0:T(8,128)S(1)} %get-tuple-element.458, pred[384,1152]{1,0:T(8,128)(4,1)S(1)} %copy-done.3), kind=kLoop, calls=%fused_computation.3 | loop fusion | flops 21227520 | bytes 28803072 | tf_op jit(solution)/shard_map/reduce_sum | solution.py:107
  245.3 13.1 %fusion.51 = bf16[16,80,384]{2,1,0:T(8,128)(2,1)} fusion(bf16[1152,16,80]{0,2,1:T(8,128)(2,1)S(1)} %bitcast.665, f32[16,384,1152]{2,1,0:T(8,128)} %get-tuple-element.459, f32[16,384]{1,0:T(8,128)S(1)} %log_add_fusion, pred[384,1152]{1,0:T(8,128)(4,1)S(1)} %copy-done.3), kind=kOutput, calls=%fused_computation.96 | convolution fusion | flops 1154187264 | bytes 32710656 | tf_op jit(solution)/shard_map/htk,khd->thd/dot_general | solution.py:110
  289.8 24.5 %multiply_reduce_fusion = (f32[16,384]{1,0:T(8,128)S(1)}, f32[16,384,1152]{2,1,0:T(8,128)}) fusion(f32[16,384,1152]{2,1,0:T(8,128)} %get-tuple-element.459, f32[16,384]{1,0:T(8,128)S(1)} %log_add_fusion, pred[384,1152]{1,0:T(8,128)(4,1)} %fusion.50, bf16[384,16,80]{0,2,1:T(8,128)(2,1)} %bitcast.669, bf16[1152,16,80]{0,2,1:T(8,128)(2,1)} %bitcast.664), kind=kOutput, calls=%fused_computation.1 | convolution fusion | flops 1160767488 | bytes 61046784 | tf_op jit(solution)/shard_map/thd,khd->htk/dot_general | solution.py:139
  314.3 23.7 %multiply_convert_fusion = bf16[16,384,1152]{2,1,0:T(8,128)(2,1)} fusion(f32[16,384,1152]{2,1,0:T(8,128)} %get-tuple-element.464, f32[16,384,1152]{2,1,0:T(8,128)} %get-tuple-element.459, f32[16,384]{1,0:T(8,128)S(1)} %get-tuple-element.463, f32[16,384]{1,0:T(8,128)S(1)} %log_add_fusion, pred[384,1152]{1,0:T(8,128)(4,1)} %fusion.50), kind=kLoop, calls=%fused_computation | loop fusion | flops 35389440 | bytes 71270400 | tf_op jit(solution)/shard_map/convert_element_type | solution.py:141
  354.1 14.2 %fusion.9 = bf16[1152,16,80]{0,2,1:T(8,128)(2,1)S(1)} fusion(bf16[384,16,80]{0,2,1:T(8,128)(2,1)} %bitcast.670, f32[16,384,1152]{2,1,0:T(8,128)} %get-tuple-element.459, f32[16,384]{1,0:T(8,128)S(1)} %log_add_fusion, pred[384,1152]{1,0:T(8,128)(4,1)} %fusion.50), kind=kOutput, calls=%fused_computation.23 | convolution fusion | flops 1155170304 | bytes 32710656 | tf_op jit(solution)/shard_map/htk,thd->khd/dot_general | solution.py:142
  380.8 11.7 fusion.44
  401.2 24.4 %reduce-scatter.11.cloned.1.call-done = bf16[256,1280]{1,0:T(8,128)(2,1)} async-done(((bf16[1024,1280]{1,0:T(8,128)(2,1)}), bf16[256,1280]{1,0:T(8,128)(2,1)}) %reduce-scatter.11.cloned.1.call-update) | async-done | bytes 655376 | tf_op jit(solution)/shard_map/reduce_scatter | solution.py:155
  442.1 17.9 %convolution_convert_fusion = bf16[6,1280,1280]{2,1,0:T(8,128)(2,1)} fusion(bf16[6,384,1280]{2,1,0:T(8,128)(2,1)} %get-tuple-element.466, bf16[6,384,1280]{2,1,0:T(8,128)(2,1)} %bitcast_dynamic-update-slice_fusion), kind=kOutput, calls=%fused_computation.4 | convolution fusion | flops 7559577600 | bytes 31457280 | tf_op jit(solution)/shard_map/mto,mti->omi/dot_general | solution.py:172
  460.0 26.4 %copy.101 = bf16[1280,7680]{1,0:T(8,128)(2,1)} copy(bf16[1280,7680]{0,1:T(8,128)(2,1)} %bitcast.668) | data formatting | bytes 39321600
  497.8 131.3 %reduce-scatter.13.cloned.1.call-done = bf16[320,7680]{1,0:T(8,128)(2,1)} async-done(((bf16[1280,7680]{1,0:T(8,128)(2,1)}), bf16[320,7680]{1,0:T(8,128)(2,1)}) %reduce-scatter.13.cloned.1.call-update) | async-done | bytes 4915216
  656.0 10.7 convolution_bitcast_fusion
  671.0 68.0 %all-reduce.5.cloned.1.call-done = (f32[320,8]{0,1:T(8,128)}, f32[320,8]{0,1:T(8,128)}, f32[320,8]{0,1:T(8,128)}, f32[320,8]{0,1:T(8,128)}, f32[320,8]{0,1:T(8,128)}, /*index=5*/f32[320,8]{0,1:T(8,128)}, f32[5,320]{1,0:T(8,128)}) async-done(((f32[320,8]{0,1:T(8,128)}, f32[320,8]{0,1:T(8,128)}, f32[320,8]{0,1:T(8,128)}, f32[320,8]{0,1:T(8,128)}, f32[320,8]{0,1:T(8,128)}, /*index=5*/f32[320,8]{0,1:T(8,128)}, ...) | async-done | bytes 67856 | tf_op jit(solution)/shard_map/psum | solution.py:198
  780.5 17.7 %subtract_multiply_fusion.35 = (f32[320,1,1]{0,2,1:T(1,128)S(1)}, f32[320,1,1]{0,2,1:T(1,128)S(1)}, f32[320,1,1]{0,2,1:T(1,128)S(1)}, f32[320,1,1]{0,2,1:T(1,128...) fusion(f32[320,1,1]{0,2,1:T(1,128)S(1)} %get-tuple-element.437, ...), kind=kLoop, calls=%fused_computation.622 | loop fusion | flops 20160 | bytes 19340 | tf_op jit(solution)/shard_map/mul | solution.py:32
  842.7 17.6 %subtract_multiply_fusion.28 = (f32[320,1,1]{0,2,1:T(1,128)S(1)}, f32[320,1,1]{0,2,1:T(1,128)S(1)}, f32[320,1,1]{0,2,1:T(1,128)S(1)}, f32[320,1,1]{0,2,1:T(1,128...) fusion(f32[320,1,1]{0,2,1:T(1,128)S(1)} %get-tuple-element.404, ...), kind=kLoop, calls=%fused_computation.566 | loop fusion | flops 20160 | bytes 19340 | tf_op jit(solution)/shard_map/mul | solution.py:32
  904.0 17.6 %subtract_multiply_fusion.21 = (f32[320,1,1]{0,2,1:T(1,128)S(1)}, f32[320,1,1]{0,2,1:T(1,128)S(1)}, f32[320,1,1]{0,2,1:T(1,128)S(1)}, f32[320,1,1]{0,2,1:T(1,128...) fusion(f32[320,1,1]{0,2,1:T(1,128)S(1)} %get-tuple-element.371, ...), kind=kLoop, calls=%fused_computation.510 | loop fusion | flops 20160 | bytes 19340 | tf_op jit(solution)/shard_map/mul | solution.py:32
  965.4 17.6 %subtract_multiply_fusion.14 = (f32[320,1,1]{0,2,1:T(1,128)S(1)}, f32[320,1,1]{0,2,1:T(1,128)S(1)}, f32[320,1,1]{0,2,1:T(1,128)S(1)}, f32[320,1,1]{0,2,1:T(1,128...) fusion(f32[320,1,1]{0,2,1:T(1,128)S(1)} %get-tuple-element.338, ...), kind=kLoop, calls=%fused_computation.454 | loop fusion | flops 20160 | bytes 19340 | tf_op jit(solution)/shard_map/mul | solution.py:32
  1026.8 17.6 %subtract_multiply_fusion.7 = (f32[320,1,1]{0,2,1:T(1,128)S(1)}, f32[320,1,1]{0,2,1:T(1,128)S(1)}, f32[320,1,1]{0,2,1:T(1,128)S(1)}, f32[320,1,1]{0,2,1:T(1,128)...) fusion(f32[320,1,1]{0,2,1:T(1,128)S(1)} %get-tuple-element.305, ...), kind=kLoop, calls=%fused_computation.398 | loop fusion | flops 20160 | bytes 19340 | tf_op jit(solution)/shard_map/mul | solution.py:32
  1088.3 17.5 %subtract_multiply_fusion = (f32[320,1,1]{0,2,1:T(1,128)S(1)}, f32[320,1,1]{0,2,1:T(1,128)S(1)}, f32[320,1,1]{0,2,1:T(1,128)S(1)}, f32[320,1,1]{0,2,1:T(1,128)S(...) fusion(f32[320,1,1]{0,2,1:T(1,128)S(1)} %get-tuple-element.272, f32[]{:T(128)S(6)} %rsqrt.263, ...), kind=kLoop, calls=%fused_computation.342 | loop fusion | flops 20160 | bytes 19340 | tf_op jit(solution)/shard_map/mul | solution.py:32
  1109.5 71.6 %all-reduce.7.cloned.1.call-done = (bf16[1,1280,8]{1,2,0:T(8,128)(2,1)}, bf16[1,1280,8]{1,2,0:T(8,128)(2,1)}, bf16[1,1280,8]{1,2,0:T(8,128)(2,1)}, bf16[1,1280,8...) async-done(((bf16[1,1280,8]{1,2,0:T(8,128)(2,1)}, bf16[1,1280,8]{1,2,0:T(8,128)(2,1)}, bf16[1,1280,8]{1,2,0:T(8,128)(2,1)}, ...) | async-done | bytes 122896 | tf_op jit(solution)/shard_map/psum | solution.py:203
  1185.5 12.8 %bitcast_subtract_fusion = (f32[320,6,1280]{2,0,1:T(8,128)}, f32[6,1280,320]{1,2,0:T(8,128)S(1)}) fusion(f32[320,6,1280]{2,0,1:T(8,128)} %convert_add_fusion, f32[6,1280,8]{1,2,0:T(8,128)S(1)} %convert_multiply_fusion.5, f32[320,6,8]{0,2,1:T(8,128)S(1)} %constant_dynamic-update-slice_fusion.8), kind=kOutput, calls=%fused_computation.7 | convolution fusion | flops 238387200 | bytes 29798400 | tf_op jit(solution)/shard_map/upt,pqt->upq/dot_general | solution.py:208
  (304 shorter events, 424.6 us)
Async XLA Ops:
  7.2 648.8 %copy-start = (f32[6,1280,8]{1,2,0:T(8,128)S(1)}, f32[6,1280,8]{1,2,0:T(8,128)}, u32[]{:S(2)}) copy-start(f32[6,1280,8]{1,2,0:T(8,128)} %param.14) | copy-start | bytes 737284
  7.2 129.4 %all-gather.7.cloned.1.call-start = ((), (), s32[]{:S(2)}) async-start(), calls=%async_computation.4 | async-start | bytes 24576000 | tf_op jit(solution)/shard_map/all_gather | solution.py:59
  7.9 167.5 %all-gather.9.cloned.1.call-start = ((), (), s32[]{:S(2)}) async-start(), calls=%async_computation.7 | async-start | bytes 3276800 | tf_op jit(solution)/shard_map/all_gather | solution.py:80
  14.3 132.7 %copy-start.25 = (f32[1280,5]{0,1:T(8,128)}, f32[1280,5]{0,1:T(8,128)S(1)}, u32[]{:S(2)}) copy-start(f32[1280,5]{0,1:T(8,128)S(1)} %reshape.8102) | copy-start | bytes 76804
  15.0 136.4 %copy-start.26 = (f32[1280]{0:T(1024)}, f32[1280]{0:T(1024)S(1)}, u32[]{:S(2)}) copy-start(f32[1280]{0:T(1024)S(1)} %get-tuple-element.55) | copy-start | bytes 15364
  15.0 138.7 %copy-start.22 = (f32[1280]{0:T(1024)}, f32[1280]{0:T(1024)S(1)}, u32[]{:S(2)}) copy-start(f32[1280]{0:T(1024)S(1)} %get-tuple-element.58) | copy-start | bytes 15364
  15.8 137.9 %copy-start.28 = (f32[384]{0:T(512)}, f32[384]{0:T(512)S(1)}, u32[]{:S(2)}) copy-start(f32[384]{0:T(512)S(1)} %get-tuple-element.453) | copy-start | bytes 4612
  149.7 53.4 %all-gather.11.cloned.1.call-start = ((), (), s32[]{:S(2)}) async-start(), calls=%async_computation.8 | async-start | bytes 3276800 | tf_op jit(solution)/shard_map/all_gather | solution.py:79
  150.5 248.2 %reduce-scatter.9.cloned.1.call-start = ((), (), s32[]{:S(2)}) async-start(), calls=%async_computation.5 | async-start | bytes 3276800 | tf_op jit(solution)/shard_map/reduce_scatter | solution.py:152
  231.6 13.7 %copy-start.2 = (bf16[1152,1280]{0,1:T(8,128)(2,1)S(1)}, bf16[1152,1280]{0,1:T(8,128)(2,1)}, u32[]{:S(2)}) copy-start(bf16[1152,1280]{0,1:T(8,128)(2,1)} %copy.80) | copy-start | bytes 8847364
  264.9 16.4 %copy-start.9 = (f32[384,1280]{1,0:T(8,128)}, f32[384,1280]{1,0:T(8,128)S(1)}, u32[]{:S(2)}) copy-start(f32[384,1280]{1,0:T(8,128)S(1)} %get-tuple-element.461) | copy-start | bytes 5898244
  354.0 71.6 %reduce-scatter.11.cloned.1.call-start = ((), (), s32[]{:S(2)}) async-start(), calls=%async_computation.6 | async-start | bytes 3276800 | tf_op jit(solution)/shard_map/reduce_scatter | solution.py:155
  376.2 119.9 %reduce-scatter.15.cloned.1.call-start = ((), (), s32[]{:S(2)}) async-start(), calls=%async_computation.10 | async-start | bytes 819200
  397.3 28.3 %copy-start.14 = (bf16[1,128,1280]{2,1,0:T(8,128)(2,1)S(1)}, bf16[1,128,1280]{2,1,0:T(8,128)(2,1)}, u32[]{:S(2)}) copy-start(bf16[1,128,1280]{2,1,0:T(8,128)(2,1)} %copy.88) | copy-start | bytes 983044
  398.7 29.2 %copy-start.6 = (f32[384,1280]{1,0:T(8,128)S(1)}, f32[384,1280]{1,0:T(8,128)}, u32[]{:S(2)}) copy-start(f32[384,1280]{1,0:T(8,128)} %copy-done.5) | copy-start | bytes 5898244
  442.1 187.0 %reduce-scatter.13.cloned.1.call-start = ((), (), s32[]{:S(2)}) async-start(), calls=%async_computation.9 | async-start | bytes 24576000
  486.4 252.5 %all-reduce.5.cloned.1.call-start = ((), (), s32[]{:S(2)}) async-start(), calls=%async_computation.11 | async-start | bytes 172032 | tf_op jit(solution)/shard_map/psum | solution.py:198
  667.3 513.8 %all-reduce.7.cloned.1.call-start = ((), (), s32[]{:S(2)}) async-start(), calls=%async_computation.12 | async-start | bytes 245760 | tf_op jit(solution)/shard_map/psum | solution.py:203
  739.0 124.4 %copy-start.34 = (f32[320,8]{0,1:T(8,128)S(1)}, f32[320,8]{0,1:T(8,128)}, u32[]{:S(2)}) copy-start(f32[320,8]{0,1:T(8,128)} %get-tuple-element.223) | copy-start | bytes 30724
  798.1 126.5 %copy-start.33 = (f32[320,8]{0,1:T(8,128)S(1)}, f32[320,8]{0,1:T(8,128)}, u32[]{:S(2)}) copy-start(f32[320,8]{0,1:T(8,128)} %get-tuple-element.224) | copy-start | bytes 30724
  860.3 125.8 %copy-start.32 = (f32[320,8]{0,1:T(8,128)S(1)}, f32[320,8]{0,1:T(8,128)}, u32[]{:S(2)}) copy-start(f32[320,8]{0,1:T(8,128)} %get-tuple-element.225) | copy-start | bytes 30724
  921.6 125.8 %copy-start.31 = (f32[320,8]{0,1:T(8,128)S(1)}, f32[320,8]{0,1:T(8,128)}, u32[]{:S(2)}) copy-start(f32[320,8]{0,1:T(8,128)} %get-tuple-element.226) | copy-start | bytes 30724
  983.0 125.8 %copy-start.35 = (f32[5,320]{1,0:T(8,128)S(1)}, f32[5,320]{1,0:T(8,128)}, u32[]{:S(2)}) copy-start(f32[5,320]{1,0:T(8,128)} %param.16) | copy-start | bytes 19204
  983.1 125.8 %copy-start.36 = (f32[5,320]{1,0:T(8,128)S(1)}, f32[5,320]{1,0:T(8,128)}, u32[]{:S(2)}) copy-start(f32[5,320]{1,0:T(8,128)} %get-tuple-element.227) | copy-start | bytes 19204
  (29 other events, 137.0 us)
Sparse Core Ops, SparseCore 0:
  9.6 126.9 all-gather.6
  149.9 25.5 all-gather.8
  177.6 25.5 all-gather.10
  354.1 34.4 reduce-scatter.8
  391.1 34.5 reduce-scatter.10
  442.2 22.4 reduce-scatter.14
  486.6 142.4 reduce-scatter.12
  667.5 71.4 all-reduce.4
  1109.6 71.4 all-reduce.6
where the time goes:
time: 1230 us; the launch traced here: 1220 us
  waiting for transfers between devices  457 us (37%)
  other arithmetic  393 us (32%)
  matrix products  192 us (16%)
  local copies, waits for them, and re-layouts  118 us (10%)
  between operations  47.3 us (4%)
    reduce_sum x60, other arithmetic, orthonormal(): jnp.sum(earlier * column, axis=-2, keepdims=True) * earlier  164 us
    unnamed x11, waiting for transfers between devices  133 us
    all_gather x1, waiting for transfers between devices, on_device(): lax.all_gather(weights, 'zero', axis=0, tiled=True)  121 us
    mul x6, other arithmetic, orthonormal(): column * lax.rsqrt(jnp.sum(column * column, axis=-2, keepdims=True) + EPS)  106 us
    psum x1, waiting for transfers between devices, on_device(): lax.psum(right_term.astype(jnp.bfloat16), 'rep').astype(jnp.float32)  71.6 us
    psum x1, waiting for transfers between devices, on_device(): left_sum = lax.psum(local_left_factor[:, mat_index], 'rep')  68 us
    unnamed x106, local copies, waits for them, and re-layouts  62 us
    reduce_sum x30, other arithmetic, orthonormal(): jnp.sum(column * column, axis=-2, keepdims=True) + EPS  49.2 us
  transfers between devices with their start and end apart: 9, of which 7 were waited for; matrix products, arithmetic and copies ran while one was open for 9% of the time, Pallas kernels for 0%

commit v1 on v0

--- a/solution.py
+++ b/solution.py
@@ -11,6 +11,28 @@
 LOG2E = 1.442695041
 NEG = -1e30
 PRECISION_HIGH = lax.Precision.HIGHEST
+
+
+def laid_out(parts, dim):
+    parts = jnp.moveaxis(parts, 0, dim)
+    shape = parts.shape
+    return parts.reshape(*shape[:dim], shape[dim] * shape[dim + 1], *shape[dim + 2 :])
+
+
+def collect(x, axis, dim):
+    count = lax.axis_size(axis)
+    pairs = [(i, (i + 1) % count) for i in range(count)]
+    back = [(b, a) for a, b in pairs]
+    lower, upper = ([], [])
+    for step in range(count - 1):
+        if step % 2 == 0:
+            lower.append(lax.ppermute(lower[-1] if lower else x, axis, pairs))
+        else:
+            upper.append(lax.ppermute(upper[-1] if upper else x, axis, back))
+    blocks = jnp.stack([*lower[::-1], x, *upper])
+    shift = lax.axis_index(axis) - len(lower)
+    blocks = blocks[(jnp.arange(count) - shift) % count]
+    return laid_out(blocks, dim)
 
 
 def rms_scale(field):
@@ -56,7 +78,7 @@
     prompt_rows = PROMPT // zero_count
     prompt_valid = prompt_len[0]
     full_w, full_v = (
-        lax.all_gather(weights, "zero", axis=0, tiled=True),
+        collect(weights, "zero", 0),
         lax.all_gather(vectors, "zero", axis=1, tiled=True),
     )
     vec_float = full_v.astype(f32)

time: 1230 us -> 1380 us (1.12)
  waiting for transfers between devices: 457 us -> 510 us
  blocking collectives: 6.25 us -> 54.4 us
  other arithmetic: 393 us -> 418 us
  local copies, waits for them, and re-layouts: 118 us -> 137 us
    ppermute x0 -> x3, waiting for transfers between devices: none -> 104 us  [the longest x2 104 us: collect(): lower.append(lax.ppermute(lower[-1] if lower else x, axis, pairs))]
    all_gather x1, blocking collectives: 6.25 us -> 54.4 us  [on_device(): lax.all_gather(vectors, 'zero', axis=1, tiled=True)]
    all_gather x1, waiting for transfers between devices: 121 us -> 92.3 us  [on_device(): back_w = lax.all_gather(weights, 'zero', axis=0, tiled=True)]
    gather x0 -> x4, local copies, waits for them, and re-layouts: none -> 26.2 us  [collect(): blocks = blocks[(jnp.arange(count) - shift) % count]]
    unnamed x106 -> x117, local copies, waits for them, and re-layouts: 62 us -> 67.9 us
  transfers between devices with their start and end apart: 9 -> 12, of which waited for: 7 -> 8; matrix products, arithmetic and copies ran while one was open for 9% -> 13% of each run, Pallas kernels for 0% -> 0%
where the time goes in v1:
time: 1380 us; the launch traced here: 1370 us
  waiting for transfers between devices  510 us (37%)
  other arithmetic  418 us (30%)
  matrix products  196 us (14%)
  local copies, waits for them, and re-layouts  137 us (10%)
  blocking collectives  54.4 us (4%)
  between operations  47.1 us (3%)
    reduce_sum x60, other arithmetic, orthonormal(): jnp.sum(earlier * column, axis=-2, keepdims=True) * earlier  164 us
    unnamed x11, waiting for transfers between devices  133 us
    mul x6, other arithmetic, orthonormal(): column * lax.rsqrt(jnp.sum(column * column, axis=-2, keepdims=True) + EPS)  106 us
    ppermute x2, waiting for transfers between devices, collect(): lower.append(lax.ppermute(lower[-1] if lower else x, axis, pairs))  104 us
    all_gather x1, waiting for transfers between devices, on_device(): back_w = lax.all_gather(weights, 'zero', axis=0, tiled=True)  92.3 us
    psum x1, waiting for transfers between devices, on_device(): lax.psum(right_term.astype(jnp.bfloat16), 'rep').astype(jnp.float32)  71.6 us
    psum x1, waiting for transfers between devices, on_device(): left_sum = lax.psum(local_left_factor[:, mat_index], 'rep')  68 us
    unnamed x117, local copies, waits for them, and re-layouts  67.9 us
  transfers between devices with their start and end apart: 12, of which 8 were waited for; matrix products, arithmetic and copies ran while one was open for 13% of the time, Pallas kernels for 0%

profile of v1, /device:TPU:0, one launch (start us, length us, event | category | flops | bytes accessed | tf_op | source)
XLA Modules:
  0.0 1369.3 jit_solution(4995776968461002093)
XLA Ops:
  9.8 104.2 %collective-permute-done = bf16[320,6,1280]{2,0,1:T(8,128)(2,1)} collective-permute-done((bf16[320,6,1280]{2,0,1:T(8,128)(2,1)}, bf16[320,6,1280]{2,0,1:T(8,128)(2,1)}, u32[]{:S(2)}, u32[]{:S(2)}) %collective-permute-start) | collective-permute-done | bytes 4915232 | tf_op jit(solution)/shard_map/ppermute | solution.py:29
  116.4 54.4 %all-gather.2 = bf16[4,320,5]{1,2,0:T(8,128)(2,1)S(1)} all-gather(bf16[1,320,5]{1,2,0:T(8,128)(2,1)} %bitcast.721), channel_id=1, replica_groups=mesh['rep'=8,'zero'=4] {'zero'}, dimensions={0}, use_global_device_ids=true | all-gather | bytes 16000 | tf_op jit(solution)/shard_map/all_gather | solution.py:82
  253.1 18.4 %all-gather.11.cloned.1.call-done = bf16[1,1024,1280]{1,2,0:T(8,128)(2,1)} async-done(((bf16[1,256,1280]{1,2,0:T(8,128)(2,1)}), bf16[1,1024,1280]{1,2,0:T(8,128)(2,1)}) %all-gather.11.cloned.1.call-update) | async-done | bytes 2621456 | tf_op jit(solution)/shard_map/all_gather | solution.py:101
  273.7 12.2 select_reduce_fusion
  285.8 13.5 exponential_reduce_fusion
  301.6 17.5 %fusion.53 = bf16[16,80,384]{2,1,0:T(8,128)(2,1)} fusion(bf16[1152,16,80]{0,2,1:T(8,128)(2,1)S(1)} %bitcast.694, f32[16,384,1152]{2,1,0:T(8,128)} %get-tuple-element.461, f32[16,384]{1,0:T(8,128)S(1)} %log_add_fusion, pred[384,1152]{1,0:T(8,128)(4,1)S(1)} %copy-done.5), kind=kOutput, calls=%fused_computation.107 | convolution fusion | flops 1154187264 | bytes 32710656 | tf_op jit(solution)/shard_map/htk,khd->thd/dot_general | solution.py:132
  333.0 92.3 %all-gather.7.cloned.1.call-done = bf16[1280,6,1280]{2,0,1:T(8,128)(2,1)} async-done(((bf16[320,6,1280]{2,0,1:T(8,128)(2,1)}), bf16[1280,6,1280]{2,0,1:T(8,128)(2,1)}) %all-gather.7.cloned.1.call-update) | async-done | bytes 19660816 | tf_op jit(solution)/shard_map/all_gather | solution.py:146
  444.3 24.5 %multiply_reduce_fusion = (f32[16,384]{1,0:T(8,128)S(1)}, f32[16,384,1152]{2,1,0:T(8,128)}) fusion(f32[16,384,1152]{2,1,0:T(8,128)} %get-tuple-element.461, f32[16,384]{1,0:T(8,128)S(1)} %log_add_fusion, pred[384,1152]{1,0:T(8,128)(4,1)} %fusion.52, bf16[384,16,80]{0,2,1:T(8,128)(2,1)} %bitcast.703, bf16[1152,16,80]{0,2,1:T(8,128)(2,1)} %bitcast.695), kind=kOutput, calls=%fused_computation.4 | convolution fusion | flops 1160767488 | bytes 61046784 | tf_op jit(solution)/shard_map/thd,khd->htk/dot_general | solution.py:161
  468.8 23.5 %multiply_convert_fusion = bf16[16,384,1152]{2,1,0:T(8,128)(2,1)} fusion(f32[16,384,1152]{2,1,0:T(8,128)} %get-tuple-element.466, f32[16,384,1152]{2,1,0:T(8,128)} %get-tuple-element.461, f32[16,384]{1,0:T(8,128)S(1)} %get-tuple-element.465, f32[16,384]{1,0:T(8,128)S(1)} %log_add_fusion, pred[384,1152]{1,0:T(8,128)(4,1)} %fusion.52), kind=kLoop, calls=%fused_computation.3 | loop fusion | flops 35389440 | bytes 71270400 | tf_op jit(solution)/shard_map/convert_element_type | solution.py:163
  508.4 14.2 %fusion.4 = bf16[1152,16,80]{0,2,1:T(8,128)(2,1)S(1)} fusion(bf16[384,16,80]{0,2,1:T(8,128)(2,1)} %bitcast.704, f32[16,384,1152]{2,1,0:T(8,128)} %get-tuple-element.461, f32[16,384]{1,0:T(8,128)S(1)} %log_add_fusion, pred[384,1152]{1,0:T(8,128)(4,1)} %fusion.52), kind=kOutput, calls=%fused_computation.27 | convolution fusion | flops 1155170304 | bytes 32710656 | tf_op jit(solution)/shard_map/htk,thd->khd/dot_general | solution.py:164
  534.3 11.7 fusion.46
  557.1 22.9 %reduce-scatter.11.cloned.1.call-done = bf16[256,1280]{1,0:T(8,128)(2,1)} async-done(((bf16[1024,1280]{1,0:T(8,128)(2,1)}), bf16[256,1280]{1,0:T(8,128)(2,1)}) %reduce-scatter.11.cloned.1.call-update) | async-done | bytes 655376 | tf_op jit(solution)/shard_map/reduce_scatter | solution.py:177
  596.4 17.9 %convolution_convert_fusion = bf16[6,1280,1280]{2,1,0:T(8,128)(2,1)} fusion(bf16[6,384,1280]{2,1,0:T(8,128)(2,1)} %get-tuple-element.468, bf16[6,384,1280]{2,1,0:T(8,128)(2,1)} %bitcast_dynamic-update-slice_fusion), kind=kOutput, calls=%fused_computation.7 | convolution fusion | flops 7559577600 | bytes 31457280 | tf_op jit(solution)/shard_map/mto,mti->omi/dot_general | solution.py:194
  614.3 26.4 %copy.90 = bf16[1280,7680]{1,0:T(8,128)(2,1)} copy(bf16[1280,7680]{0,1:T(8,128)(2,1)} %bitcast.702) | data formatting | bytes 39321600
  651.9 131.4 %reduce-scatter.13.cloned.1.call-done = bf16[320,7680]{1,0:T(8,128)(2,1)} async-done(((bf16[1280,7680]{1,0:T(8,128)(2,1)}), bf16[320,7680]{1,0:T(8,128)(2,1)}) %reduce-scatter.13.cloned.1.call-update) | async-done | bytes 4915216
  825.2 68.0 %all-reduce.5.cloned.1.call-done = (f32[320,8]{0,1:T(8,128)}, f32[320,8]{0,1:T(8,128)}, f32[320,8]{0,1:T(8,128)}, f32[320,8]{0,1:T(8,128)}, f32[320,8]{0,1:T(8,128)}, /*index=5*/f32[320,8]{0,1:T(8,128)}, f32[5,320]{1,0:T(8,128)}) async-done(((f32[320,8]{0,1:T(8,128)}, f32[320,8]{0,1:T(8,128)}, f32[320,8]{0,1:T(8,128)}, f32[320,8]{0,1:T(8,128)}, f32[320,8]{0,1:T(8,128)}, /*index=5*/f32[320,8]{0,1:T(8,128)}, ...) | async-done | bytes 67856 | tf_op jit(solution)/shard_map/psum | solution.py:220
  934.8 17.7 %subtract_multiply_fusion.35 = (f32[320,1,1]{0,2,1:T(1,128)S(1)}, f32[320,1,1]{0,2,1:T(1,128)S(1)}, f32[320,1,1]{0,2,1:T(1,128)S(1)}, f32[320,1,1]{0,2,1:T(1,128...) fusion(f32[320,1,1]{0,2,1:T(1,128)S(1)} %get-tuple-element.437, ...), kind=kLoop, calls=%fused_computation.638 | loop fusion | flops 20160 | bytes 19340 | tf_op jit(solution)/shard_map/mul | solution.py:54
  997.0 17.6 %subtract_multiply_fusion.28 = (f32[320,1,1]{0,2,1:T(1,128)S(1)}, f32[320,1,1]{0,2,1:T(1,128)S(1)}, f32[320,1,1]{0,2,1:T(1,128)S(1)}, f32[320,1,1]{0,2,1:T(1,128...) fusion(f32[320,1,1]{0,2,1:T(1,128)S(1)} %get-tuple-element.404, ...), kind=kLoop, calls=%fused_computation.582 | loop fusion | flops 20160 | bytes 19340 | tf_op jit(solution)/shard_map/mul | solution.py:54
  1058.3 17.6 %subtract_multiply_fusion.21 = (f32[320,1,1]{0,2,1:T(1,128)S(1)}, f32[320,1,1]{0,2,1:T(1,128)S(1)}, f32[320,1,1]{0,2,1:T(1,128)S(1)}, f32[320,1,1]{0,2,1:T(1,128...) fusion(f32[320,1,1]{0,2,1:T(1,128)S(1)} %get-tuple-element.371, ...), kind=kLoop, calls=%fused_computation.526 | loop fusion | flops 20160 | bytes 19340 | tf_op jit(solution)/shard_map/mul | solution.py:54
  1119.7 17.6 %subtract_multiply_fusion.14 = (f32[320,1,1]{0,2,1:T(1,128)S(1)}, f32[320,1,1]{0,2,1:T(1,128)S(1)}, f32[320,1,1]{0,2,1:T(1,128)S(1)}, f32[320,1,1]{0,2,1:T(1,128...) fusion(f32[320,1,1]{0,2,1:T(1,128)S(1)} %get-tuple-element.338, ...), kind=kLoop, calls=%fused_computation.470 | loop fusion | flops 20160 | bytes 19340 | tf_op jit(solution)/shard_map/mul | solution.py:54
  1181.1 17.6 %subtract_multiply_fusion.7 = (f32[320,1,1]{0,2,1:T(1,128)S(1)}, f32[320,1,1]{0,2,1:T(1,128)S(1)}, f32[320,1,1]{0,2,1:T(1,128)S(1)}, f32[320,1,1]{0,2,1:T(1,128)...) fusion(f32[320,1,1]{0,2,1:T(1,128)S(1)} %get-tuple-element.305, ...), kind=kLoop, calls=%fused_computation.414 | loop fusion | flops 20160 | bytes 19340 | tf_op jit(solution)/shard_map/mul | solution.py:54
  1242.6 17.5 %subtract_multiply_fusion = (f32[320,1,1]{0,2,1:T(1,128)S(1)}, f32[320,1,1]{0,2,1:T(1,128)S(1)}, f32[320,1,1]{0,2,1:T(1,128)S(1)}, f32[320,1,1]{0,2,1:T(1,128)S(...) fusion(f32[320,1,1]{0,2,1:T(1,128)S(1)} %get-tuple-element.272, f32[]{:T(128)S(6)} %rsqrt.263, ...), kind=kLoop, calls=%fused_computation.358 | loop fusion | flops 20160 | bytes 19340 | tf_op jit(solution)/shard_map/mul | solution.py:54
  1263.8 71.6 %all-reduce.7.cloned.1.call-done = (bf16[1,1280,8]{1,2,0:T(8,128)(2,1)}, bf16[1,1280,8]{1,2,0:T(8,128)(2,1)}, bf16[1,1280,8]{1,2,0:T(8,128)(2,1)}, bf16[1,1280,8...) async-done(((bf16[1,1280,8]{1,2,0:T(8,128)(2,1)}, bf16[1,1280,8]{1,2,0:T(8,128)(2,1)}, bf16[1,1280,8]{1,2,0:T(8,128)(2,1)}, ...) | async-done | bytes 122896 | tf_op jit(solution)/shard_map/psum | solution.py:225
  1339.8 12.8 bitcast_subtract_fusion
  (329 shorter events, 479.1 us)
Async XLA Ops:
  7.2 803.1 %copy-start = (f32[6,1280,8]{1,2,0:T(8,128)S(1)}, f32[6,1280,8]{1,2,0:T(8,128)}, u32[]{:S(2)}) copy-start(f32[6,1280,8]{1,2,0:T(8,128)} %param.14) | copy-start | bytes 737284
  7.2 264.3 %all-gather.11.cloned.1.call-start = ((), (), s32[]{:S(2)}) async-start(), calls=%async_computation.8 | async-start | bytes 3276800 | tf_op jit(solution)/shard_map/all_gather | solution.py:101
  7.2 106.8 %collective-permute-start = (bf16[320,6,1280]{2,0,1:T(8,128)(2,1)}, bf16[320,6,1280]{2,0,1:T(8,128)(2,1)}, u32[]{:S(2)}, u32[]{:S(2)}) collective-permute-start(bf16[320,6,1280]{2,0,1:T(8,128)(2,1)} %param.11), channel_id=1, source_target_pairs={{0,1},{1,2},{2,3},{3,0},{4,5},{5,6},{6,7},{7,4},{8,9},{9,10},{10,1... | collective-permute-start | bytes 14745608 | tf_op jit(solution)/shard_map/ppermute | solution.py:29
  7.8 166.1 %collective-permute-start.2 = (bf16[320,6,1280]{2,0,1:T(8,128)(2,1)}, bf16[320,6,1280]{2,0,1:T(8,128)(2,1)}, u32[]{:S(2)}, u32[]{:S(2)}) collective-permute-start(bf16[320,6,1280]{2,0,1:T(8,128)(2,1)} %param.11), channel_id=1, source_target_pairs={{1,0},{2,1},{3,2},{0,3},{5,4},{6,5},{7,6},{4,7},{9,8},{10,9},{11,1... | collective-permute-start | bytes 14745608 | tf_op jit(solution)/shard_map/ppermute | solution.py:31
  114.0 59.9 %collective-permute-start.1 = (bf16[320,6,1280]{2,0,1:T(8,128)(2,1)}, bf16[320,6,1280]{2,0,1:T(8,128)(2,1)}, u32[]{:S(2)}, u32[]{:S(2)}) collective-permute-start(bf16[320,6,1280]{2,0,1:T(8,128)(2,1)} %collective-permute-done), channel_id=1, source_target_pairs={{0,1},{1,2},{2,3},{3,0},{4,5},{5,6},{6,7},{7,4},{8,9},{9,10},{10,1... | collective-permute-start | bytes 14745608 | tf_op jit(solution)/shard_map/ppermute | solution.py:29
  171.7 72.7 %copy-start.30 = (f32[1280]{0:T(1024)}, f32[1280]{0:T(1024)S(1)}, u32[]{:S(2)}) copy-start(f32[1280]{0:T(1024)S(1)} %get-tuple-element.55) | copy-start | bytes 15364
  171.7 75.0 %copy-start.25 = (f32[1280]{0:T(1024)}, f32[1280]{0:T(1024)S(1)}, u32[]{:S(2)}) copy-start(f32[1280]{0:T(1024)S(1)} %get-tuple-element.58) | copy-start | bytes 15364
  173.9 72.8 %copy-start.32 = (f32[384]{0:T(512)}, f32[384]{0:T(512)S(1)}, u32[]{:S(2)}) copy-start(f32[384]{0:T(512)S(1)} %get-tuple-element.455) | copy-start | bytes 4612
  241.6 57.8 %all-gather.9.cloned.1.call-start = ((), (), s32[]{:S(2)}) async-start(), calls=%async_computation.7 | async-start | bytes 3276800 | tf_op jit(solution)/shard_map/all_gather | solution.py:102
  242.4 182.9 %all-gather.7.cloned.1.call-start = ((), (), s32[]{:S(2)}) async-start(), calls=%async_computation.4 | async-start | bytes 24576000 | tf_op jit(solution)/shard_map/all_gather | solution.py:146
  243.1 311.7 %reduce-scatter.9.cloned.1.call-start = ((), (), s32[]{:S(2)}) async-start(), calls=%async_computation.5 | async-start | bytes 3276800 | tf_op jit(solution)/shard_map/reduce_scatter | solution.py:174
  508.4 71.6 %reduce-scatter.11.cloned.1.call-start = ((), (), s32[]{:S(2)}) async-start(), calls=%async_computation.6 | async-start | bytes 3276800 | tf_op jit(solution)/shard_map/reduce_scatter | solution.py:177
  529.7 120.5 %reduce-scatter.15.cloned.1.call-start = ((), (), s32[]{:S(2)}) async-start(), calls=%async_computation.10 | async-start | bytes 819200
  549.3 30.6 %copy-start.17 = (bf16[1,128,1280]{2,1,0:T(8,128)(2,1)S(1)}, bf16[1,128,1280]{2,1,0:T(8,128)(2,1)}, u32[]{:S(2)}) copy-start(bf16[1,128,1280]{2,1,0:T(8,128)(2,1)} %copy.77) | copy-start | bytes 983044
  551.4 30.7 %copy-start.8 = (f32[384,1280]{1,0:T(8,128)S(1)}, f32[384,1280]{1,0:T(8,128)}, u32[]{:S(2)}) copy-start(f32[384,1280]{1,0:T(8,128)} %copy-done.7) | copy-start | bytes 5898244
  596.4 187.0 %reduce-scatter.13.cloned.1.call-start = ((), (), s32[]{:S(2)}) async-start(), calls=%async_computation.9 | async-start | bytes 24576000
  640.7 252.5 %all-reduce.5.cloned.1.call-start = ((), (), s32[]{:S(2)}) async-start(), calls=%async_computation.11 | async-start | bytes 172032 | tf_op jit(solution)/shard_map/psum | solution.py:220
  821.6 513.8 %all-reduce.7.cloned.1.call-start = ((), (), s32[]{:S(2)}) async-start(), calls=%async_computation.12 | async-start | bytes 245760 | tf_op jit(solution)/shard_map/psum | solution.py:225
  893.3 124.4 %copy-start.38 = (f32[320,8]{0,1:T(8,128)S(1)}, f32[320,8]{0,1:T(8,128)}, u32[]{:S(2)}) copy-start(f32[320,8]{0,1:T(8,128)} %get-tuple-element.223) | copy-start | bytes 30724
  893.3 185.7 %copy-start.37 = (f32[320,8]{0,1:T(8,128)S(1)}, f32[320,8]{0,1:T(8,128)}, u32[]{:S(2)}) copy-start(f32[320,8]{0,1:T(8,128)} %get-tuple-element.224) | copy-start | bytes 30724
  952.5 187.9 %copy-start.36 = (f32[320,8]{0,1:T(8,128)S(1)}, f32[320,8]{0,1:T(8,128)}, u32[]{:S(2)}) copy-start(f32[320,8]{0,1:T(8,128)} %get-tuple-element.225) | copy-start | bytes 30724
  1014.7 187.1 %copy-start.35 = (f32[320,8]{0,1:T(8,128)S(1)}, f32[320,8]{0,1:T(8,128)}, u32[]{:S(2)}) copy-start(f32[320,8]{0,1:T(8,128)} %get-tuple-element.226) | copy-start | bytes 30724
  1075.9 187.2 %copy-start.39 = (f32[5,320]{1,0:T(8,128)S(1)}, f32[5,320]{1,0:T(8,128)}, u32[]{:S(2)}) copy-start(f32[5,320]{1,0:T(8,128)} %param.16) | copy-start | bytes 19204
  1076.0 187.2 %copy-start.40 = (f32[5,320]{1,0:T(8,128)S(1)}, f32[5,320]{1,0:T(8,128)}, u32[]{:S(2)}) copy-start(f32[5,320]{1,0:T(8,128)} %get-tuple-element.227) | copy-start | bytes 19204
  (37 other events, 185.4 us)
Sparse Core Ops, SparseCore 0:
  241.8 29.6 all-gather.10
  273.6 25.8 all-gather.8
  301.1 124.2 all-gather.6
  508.5 34.4 reduce-scatter.8
  545.4 34.4 reduce-scatter.10
  596.5 22.4 reduce-scatter.14
  640.8 142.4 reduce-scatter.12
  821.8 71.4 all-reduce.4
  1263.9 71.4 all-reduce.6
